TPU v7x, 32 devices: a whole 2x2x4 slice. The times are simulated.
32 devices in a mesh: tm: 4 (over y, x), aux: 4 (over z), pair: 2 (over core).
Axes of the slice: x: 2, y: 2, z: 4, core: 2. Of those that a mesh axis runs over, the one named last changes fastest.
Arguments:
- factors: bfloat16 [3072, 5120], P('aux', 'pair'), may hold values from -0.078125 to 0.078125
- panel_factors: bfloat16 [256, 5120], P('aux', 'pair'), may hold values from -6 to 6
- time_weights: float32 [12, 5120], P('tm', 'pair'), may hold values from 0.2 to 2
- tile_mask: int32 [24, 40], P('aux', 'pair'), may hold values 0 or 1
- forward_table: float32 [12, 12], replicated, may hold values from -0.5 to 0.5
- screening: float32 [12, 256, 256], P('tm', 'aux'), may hold values from -0.375 to 0.375
- back_table: float32 [12, 12], replicated, may hold values from -0.5 to 0.5
Outputs:
- sigma: float32 [12, 5120], P('tm', 'pair')
All inputs are finite; a program needn't handle non-finite values. No bound on the sum of `tile_mask` on one device may be relied on, other than what follows from the above.
Results may differ from a plain program's by a relative error of at most 0.0003.
Values may be sent and summed in bfloat16 or wider, within the bound.
No kernel may reach another device: no remote copies, remote signals or barrier semaphores. Data moves between devices by JAX's collectives and lax.ppermute only.
A program may use at most 64 MiB of HBM per device.

v0:
```python
import jax
import jax.numpy as jnp
from jax import lax
from jax.sharding import PartitionSpec as P

TILE = 128


def expand_tiles(tile_mask):
    tile_rows, tile_cols = tile_mask.shape
    spread = jnp.broadcast_to(tile_mask[:, None, :, None], (tile_rows, TILE, tile_cols, TILE))
    return spread.reshape(tile_rows * TILE, tile_cols * TILE)


def body(factors, panel_factors, time_weights, tile_mask, forward_table, screening, back_table):
    highest = lax.Precision.HIGHEST
    masked = factors.astype(jnp.float32) * expand_tiles(tile_mask).astype(jnp.float32)
    panel_full = lax.all_gather(panel_factors, "aux", axis=0, tiled=True)
    panel_wide = panel_full.astype(jnp.float32)
    freq_count = screening.shape[0]
    first_freq = lax.axis_index("tm") * freq_count
    weights_all = lax.all_gather(time_weights, "tm", axis=0, tiled=True)
    table_rows = lax.dynamic_slice_in_dim(forward_table, first_freq, freq_count, 0)
    line_weights = jnp.dot(table_rows, weights_all, precision=highest)
    scaled = panel_wide[None, :, :] * line_weights[:, None, :]
    polar_line = jnp.einsum("tpk,qk->tpq", scaled, masked, precision=highest)
    polar_half = lax.psum_scatter(polar_line, "pair", scatter_dimension=2, tiled=True)
    inverse = lax.all_gather(screening, "aux", axis=1, tiled=True)
    screened = jnp.einsum("wpr,wrq->wpq", inverse, polar_half, precision=highest)
    back_cols = lax.dynamic_slice_in_dim(back_table, first_freq, freq_count, 1)
    lines_full = lax.all_gather(screened, "pair", axis=2, tiled=True)
    contracted = jnp.einsum("tpq,qk->tpk", lines_full, masked, precision=highest)
    partial_value = jnp.sum(panel_wide[None, :, :] * contracted, axis=1) * panel_full.shape[0] ** (
        -0.5
    )
    timed = jnp.dot(back_cols, partial_value, precision=highest)
    partial_value = lax.psum_scatter(timed, "tm", scatter_dimension=0, tiled=True)
    return lax.psum(partial_value, "aux")


def solution(mesh):
    placed = (
        P("aux", "pair"),
        P("aux", "pair"),
        P("tm", "pair"),
        P("aux", "pair"),
        P(),
        P("tm", "aux", None),
        P(),
    )
    return jax.shard_map(
        body, mesh=mesh, in_specs=placed, out_specs=P("tm", "pair"), check_vma=False
    )
```

profile of v0, /device:TPU:0, one launch (start us, length us, event | category | flops | bytes accessed | tf_op | source)
XLA Modules:
  0.0 203.3 jit_solution(14828435998711935432)
XLA Ops:
  6.5 0.0 copy-start
  6.5 0.0 all-gather.4.cloned.1.call-start
  6.5 0.7 all-gather.4.cloned.1.call-update
  7.3 0.0 reduce-scatter.2.cloned.1.call-start
  7.3 10.3 %all-gather = f32[4,3,2560]{2,1,0:T(4,128)S(1)} all-gather(f32[1,3,2560]{2,1,0:T(4,128)} %bitcast.22), channel_id=1, replica_groups=mesh['tm'=4,'aux'=4,'pair'=2] {'tm'}, dimensions={0}, use_global_device_ids=true | all-gather | bytes 153600 | tf_op jit(solution)/shard_map/all_gather | solution.py:22
  17.6 0.1 reshape.6
  17.7 0.7 convert_element_type.15
  18.4 0.9 fusion.11
  19.3 24.9 %all-gather.4.cloned.1.call-done = bf16[256,2560]{1,0:T(8,128)(2,1)} async-done(((bf16[64,2560]{1,0:T(8,128)(2,1)}), bf16[256,2560]{1,0:T(8,128)(2,1)}) %all-gather.4.cloned.1.call-update) | async-done | bytes 1310736 | tf_op jit(solution)/shard_map/all_gather | solution.py:18
  44.2 1.6 convert_element_type.13
  45.8 0.0 copy-start.2
  45.8 0.7 broadcast_in_dim.2
  46.5 0.0 copy-start.1
  46.5 3.7 %copy-done.1 = f32[6,128,20,128]{3,2,1,0:T(8,128)} copy-done((f32[6,128,20,128]{3,2,1,0:T(8,128)}, f32[6,128,20,128]{3,2,1,0:T(8,128)S(1)}, u32[]{:S(2)}) %copy-start.1) | copy-done | bytes 7864344
  50.2 0.0 copy-done.2
  50.2 22.1 %fusion.1 = f32[3,256,768]{2,1,0:T(8,128)} fusion(f32[96,8,20,128]{3,2,1,0:T(8,128)S(1)} %bitcast.20, bf16[768,2560]{1,0:T(8,128)(2,1)S(1)} %copy-done.2, f32[3,2560]{1,0:T(4,128)S(1)} %fusion.11, f32[256,2560]{1,0:T(8,128)S(1)} %convert_element_type.13), kind=kOutput, calls=%fused_computation.3 | convolution fusion | flops 18125291520 | bytes 16807936 | tf_op jit(solution)/shard_map/tpk,qk->tpq/dot_general | solution.py:26
  72.3 0.0 reduce-scatter.2.cloned.1.call-update
  72.3 0.0 all-gather.6.cloned.1.call-start
  72.4 18.2 %all_gather.14 = f32[3,256,256]{2,1,0:T(8,128)S(1)} all-gather(f32[3,64,256]{2,1,0:T(8,128)} %param.12), channel_id=1, replica_groups=mesh['tm'=4,'aux'=4,'pair'=2] {'aux'}, dimensions={1}, use_global_device_ids=true | all-gather | bytes 983040 | tf_op jit(solution)/shard_map/all_gather | solution.py:28
  90.6 4.4 %convolution_bitcast_fusion = f32[3,256,384]{1,2,0:T(8,128)} fusion(f32[3,256,384]{2,1,0:T(8,128)} %reduce-scatter.2.cloned.1.call-done, f32[3,256,256]{2,1,0:T(8,128)S(1)} %all_gather.14), kind=kOutput, calls=%fused_computation.7 | convolution fusion | flops 905969664 | bytes 3145728 | tf_op jit(solution)/shard_map/wpr,wrq->wpq/dot_general | solution.py:29
  94.9 0.0 all-gather.6.cloned.1.call-update
  95.0 0.0 copy-start.3
  95.0 0.0 all-reduce.3.cloned.1.call-start
  95.0 10.5 %all-gather.6.cloned.1.call-done = f32[3,256,768]{1,2,0:T(8,128)} async-done(((f32[3,256,384]{1,2,0:T(8,128)}), f32[3,256,768]{1,2,0:T(8,128)}) %all-gather.6.cloned.1.call-update) | async-done | bytes 2359312 | tf_op jit(solution)/shard_map/all_gather | solution.py:31
  105.5 25.5 %multiply_reduce_fusion = f32[3,2560]{1,0:T(4,128)S(1)} fusion(f32[3,256,768]{1,2,0:T(8,128)} %all-gather.6.cloned.1.call-done, f32[96,8,20,128]{3,2,1,0:T(8,128)} %bitcast.21, bf16[768,2560]{1,0:T(8,128)(2,1)} %param.7, f32[256,2560]{1,0:T(8,128)S(1)} %convert_element_type.13), kind=kOutput, calls=%fused_computation.2 | convolution fusion | flops 18127249408 | bytes 16807936 | tf_op jit(solution)/shard_map/tpq,qk->tpk/dot_general | solution.py:32
  131.1 0.0 copy-done
  131.1 1.0 fusion.7
  132.1 0.0 all-reduce.3.cloned.1.call-update
  132.1 0.6 dynamic-slice
  133.4 42.5 %all-reduce.3.cloned.1.call-done = f32[12,2560]{1,0:T(8,128)} async-done(((f32[12,2560]{1,0:T(8,128)}), f32[12,2560]{1,0:T(8,128)}) %all-reduce.3.cloned.1.call-update) | async-done | bytes 122896
  175.9 0.9 constant_dynamic-slice_fusion
  176.8 20.0 %psum.7 = f32[3,2560]{1,0:T(4,128)} all-reduce(f32[3,2560]{1,0:T(4,128)S(1)} %constant_dynamic-slice_fusion), channel_id=1, replica_groups=mesh['tm'=4,'aux'=4,'pair'=2] {'aux'}, use_global_device_ids=true, to_apply=%region_3.0 | all-reduce | flops 7680 | bytes 61440 | tf_op jit(solution)/shard_map/psum | solution.py:38
  (2 shorter events, 0.0 us)
Async XLA Ops:
  6.5 124.5 %copy-start = (f32[12,12]{1,0:T(8,128)S(1)}, f32[12,12]{1,0:T(8,128)}, u32[]{:S(2)}) copy-start(f32[12,12]{1,0:T(8,128)} %param.13) | copy-start | bytes 1732
  6.5 37.7 %all-gather.4.cloned.1.call-start = ((), (), s32[]{:S(2)}) async-start(), calls=%async_computation.1 | async-start | bytes 1638400 | tf_op jit(solution)/shard_map/all_gather | solution.py:18
  7.3 83.3 %reduce-scatter.2.cloned.1.call-start = ((), (), s32[]{:S(2)}) async-start(), calls=%async_computation.2 | async-start | bytes 3538944 | tf_op jit(solution)/shard_map/reduce_scatter | solution.py:27
  45.8 4.4 %copy-start.2 = (bf16[768,2560]{1,0:T(8,128)(2,1)S(1)}, bf16[768,2560]{1,0:T(8,128)(2,1)}, u32[]{:S(2)}) copy-start(bf16[768,2560]{1,0:T(8,128)(2,1)} %param.7) | copy-start | bytes 11796484
  46.5 3.7 %copy-start.1 = (f32[6,128,20,128]{3,2,1,0:T(8,128)}, f32[6,128,20,128]{3,2,1,0:T(8,128)S(1)}, u32[]{:S(2)}) copy-start(f32[6,128,20,128]{3,2,1,0:T(8,128)S(1)} %broadcast_in_dim.2) | copy-start | bytes 23592964
  72.3 33.2 %all-gather.6.cloned.1.call-start = ((), (), s32[]{:S(2)}) async-start(), calls=%async_computation.3 | async-start | bytes 3538944 | tf_op jit(solution)/shard_map/all_gather | solution.py:31
  95.0 37.2 %copy-start.3 = (u32[32]{0:T(128)S(1)}, u32[32]{0:T(128)}, u32[]{:S(2)}) copy-start(u32[32]{0:T(128)} %constant.20) | copy-start | bytes 388
  95.0 80.9 %all-reduce.3.cloned.1.call-start = ((), (), s32[]{:S(2)}) async-start(), calls=%async_computation.4 | async-start | bytes 327680
Sparse Core Ops, SparseCore 0:
  8.9 35.2 all-gather.3
  72.5 9.0 reduce-scatter.1
  95.1 10.3 all-gather.5
  132.2 43.6 all-reduce.2
where the time goes:
time: 204 us; the launch traced here: 203 us
  waiting for transfers between devices  78.7 us (39%)
  matrix products  53.9 us (26%)
  blocking collectives  48.4 us (24%)
  between operations  13.9 us (7%)
  local copies, waits for them, and re-layouts  5.96 us (3%)
  other arithmetic  2.31 us (1%)
    unnamed x5, waiting for transfers between devices  43.3 us
    dot_general x1, matrix products, body(): jnp.einsum('tpq,qk->tpk', lines_full, masked, precision=highest)  25.5 us
    all_gather x1, waiting for transfers between devices, body(): panel_full = lax.all_gather(panel_factors, 'aux', axis=0, tiled=True)  24.9 us
    dot_general x1, matrix products, body(): polar_line = jnp.einsum('tpk,qk->tpq', scaled, masked, precision=highest)  22.1 us
    psum x1, blocking collectives, body(): return lax.psum(partial_value, 'aux')  20 us
    all_gather x1, blocking collectives, body(): inverse = lax.all_gather(screening, 'aux', axis=1, tiled=True)  18.2 us
    all_gather x1, waiting for transfers between devices, body(): lines_full = lax.all_gather(screened, 'pair', axis=2, tiled=True)  10.5 us
    all_gather x1, blocking collectives, body(): weights_all = lax.all_gather(time_weights, 'tm', axis=0, tiled=True)  10.3 us
  transfers between devices with their start and end apart: 4, of which 3 were waited for; matrix products, arithmetic and copies ran while one was open for 1% of the time, Pallas kernels for 0%

commit v1 on v0

--- a/solution.py
+++ b/solution.py
@@ -15,7 +15,12 @@
 def body(factors, panel_factors, time_weights, tile_mask, forward_table, screening, back_table):
     highest = lax.Precision.HIGHEST
     masked = factors.astype(jnp.float32) * expand_tiles(tile_mask).astype(jnp.float32)
-    panel_full = lax.all_gather(panel_factors, "aux", axis=0, tiled=True)
+    ring = [panel_factors]
+    for hop in range(3):
+        ring.append(lax.ppermute(ring[-1], "aux", [(dev, (dev + 1) % 4) for dev in range(4)]))
+    panel_full = jnp.roll(
+        jnp.concatenate(ring[::-1], axis=0), (lax.axis_index("aux") + 1) * ring[0].shape[0], axis=0
+    )
     panel_wide = panel_full.astype(jnp.float32)
     freq_count = screening.shape[0]
     first_freq = lax.axis_index("tm") * freq_count

time: 204 us -> 199 us (0.975)
  waiting for transfers between devices: 78.7 us -> 73.2 us
  starting transfers between devices: 0.12 us -> 3.14 us
    all_gather x1 -> x0, waiting for transfers between devices: 24.9 us -> none  [body(): panel_full = lax.all_gather(panel_factors, 'aux', axis=0, tiled=True)]
    ppermute x0 -> x3, waiting for transfers between devices: none -> 20.6 us  [body(): lax.ppermute(ring[-1], 'aux', [(dev, (dev + 1) % 4) for dev in range(4)])]
    ppermute x0 -> x3, starting transfers between devices: none -> 3.06 us  [body(): lax.ppermute(ring[-1], 'aux', [(dev, (dev + 1) % 4) for dev in range(4)])]
    unnamed x5 -> x4, waiting for transfers between devices: 43.3 us -> 42.6 us
    unnamed x11 -> x20, local copies, waits for them, and re-layouts: 5.29 us -> 5.46 us
  transfers between devices with their start and end apart: 4 -> 6, of which waited for: 3 -> 4; matrix products, arithmetic and copies ran while one was open for 1% -> 1% of each run, Pallas kernels for 0% -> 0%
where the time goes in v1:
time: 199 us; the launch traced here: 198 us
  waiting for transfers between devices  73.2 us (37%)
  matrix products  54 us (27%)
  blocking collectives  46.9 us (24%)
  between operations  13.9 us (7%)
  local copies, waits for them, and re-layouts  6.15 us (3%)
  starting transfers between devices  3.14 us (2%)
    unnamed x4, waiting for transfers between devices  42.6 us
    dot_general x1, matrix products, body(): jnp.einsum('tpq,qk->tpk', lines_full, masked, precision=highest)  25.5 us
    dot_general x1, matrix products, body(): polar_line = jnp.einsum('tpk,qk->tpq', scaled, masked, precision=highest)  22.2 us
    ppermute x3, waiting for transfers between devices, body(): lax.ppermute(ring[-1], 'aux', [(dev, (dev + 1) % 4) for dev in range(4)])  20.6 us
    psum x1, blocking collectives, body(): return lax.psum(partial_value, 'aux')  20 us
    all_gather x1, blocking collectives, body(): inverse = lax.all_gather(screening, 'aux', axis=1, tiled=True)  18.3 us
    all_gather x1, waiting for transfers between devices, body(): lines_full = lax.all_gather(screened, 'pair', axis=2, tiled=True)  10 us
    all_gather x1, blocking collectives, body(): weights_all = lax.all_gather(time_weights, 'tm', axis=0, tiled=True)  8.62 us
  transfers between devices with their start and end apart: 6, of which 4 were waited for; matrix products, arithmetic and copies ran while one was open for 1% of the time, Pallas kernels for 0%

profile of v1, /device:TPU:0, one launch (start us, length us, event | category | flops | bytes accessed | tf_op | source)
XLA Modules:
  0.0 198.4 jit_solution(3093512476789765516)
XLA Ops:
  6.5 3.1 %collective-permute-start = (bf16[64,2560]{1,0:T(8,128)(2,1)}, bf16[64,2560]{1,0:T(8,128)(2,1)S(1)}, u32[]{:S(2)}, u32[]{:S(2)}) collective-permute-start(bf16[64,2560]{1,0:T(8,128)(2,1)} %param.8), channel_id=1, source_target_pairs={{0,2},{2,4},{4,6},{6,0},{1,3},{3,5},{5,7},{7,1},{8,10},{10,12},{12... | collective-permute-start | bytes 983048 | tf_op jit(solution)/shard_map/ppermute | solution.py:20
  9.6 10.0 %collective-permute-done = bf16[64,2560]{1,0:T(8,128)(2,1)S(1)} collective-permute-done((bf16[64,2560]{1,0:T(8,128)(2,1)}, bf16[64,2560]{1,0:T(8,128)(2,1)S(1)}, u32[]{:S(2)}, u32[]{:S(2)}) %collective-permute-start) | collective-permute-done | bytes 327712 | tf_op jit(solution)/shard_map/ppermute | solution.py:20
  19.6 0.0 collective-permute-start.1
  19.6 10.7 %collective-permute-done.1 = bf16[64,2560]{1,0:T(8,128)(2,1)S(1)} collective-permute-done((bf16[64,2560]{1,0:T(8,128)(2,1)S(1)}, bf16[64,2560]{1,0:T(8,128)(2,1)S(1)}, u32[]{:S(2)}, u32[]{:S(2)}) %collective-permute-start.1) | collective-permute-done | bytes 327712 | tf_op jit(solution)/shard_map/ppermute | solution.py:20
  30.2 0.0 collective-permute-start.2
  30.2 8.6 %all-gather = f32[4,3,2560]{2,1,0:T(4,128)S(1)} all-gather(f32[1,3,2560]{2,1,0:T(4,128)} %bitcast.22), channel_id=1, replica_groups=mesh['tm'=4,'aux'=4,'pair'=2] {'tm'}, dimensions={0}, use_global_device_ids=true | all-gather | bytes 153600 | tf_op jit(solution)/shard_map/all_gather | solution.py:27
  38.9 0.1 reshape.6
  38.9 0.7 convert_element_type.15
  39.6 0.9 fusion.11
  40.5 0.0 collective-permute-done.2
  40.8 0.3 dynamic-slice_convert_fusion
  41.1 0.0 copy-start.2
  41.1 0.7 broadcast_in_dim.2
  41.8 3.7 %copy-done.1 = f32[6,128,20,128]{3,2,1,0:T(8,128)} copy-done((f32[6,128,20,128]{3,2,1,0:T(8,128)}, f32[6,128,20,128]{3,2,1,0:T(8,128)S(1)}, u32[]{:S(2)}) %copy-start.1) | copy-done | bytes 7864344
  45.5 22.2 %fusion.1 = f32[3,256,768]{2,1,0:T(8,128)} fusion(f32[96,8,20,128]{3,2,1,0:T(8,128)S(1)} %bitcast.20, bf16[768,2560]{1,0:T(8,128)(2,1)S(1)} %copy-done.2, f32[3,2560]{1,0:T(4,128)S(1)} %fusion.11, f32[256,2560]{1,0:T(8,128)S(1)} %dynamic-slice_convert_fusion), kind=kOutput, calls=%fused_computation.3 | convolution fusion | flops 18125291520 | bytes 16807936 | tf_op jit(solution)/shard_map/tpk,qk->tpq/dot_general | solution.py:31
  67.7 0.0 reduce-scatter.2.cloned.1.call-update
  67.7 0.0 all-gather.3.cloned.1.call-start
  67.8 18.3 %all_gather.10 = f32[3,256,256]{2,1,0:T(8,128)S(1)} all-gather(f32[3,64,256]{2,1,0:T(8,128)} %param.12), channel_id=1, replica_groups=mesh['tm'=4,'aux'=4,'pair'=2] {'aux'}, dimensions={1}, use_global_device_ids=true | all-gather | bytes 983040 | tf_op jit(solution)/shard_map/all_gather | solution.py:33
  86.1 4.3 %convolution_bitcast_fusion = f32[3,256,384]{1,2,0:T(8,128)} fusion(f32[3,256,384]{2,1,0:T(8,128)} %reduce-scatter.2.cloned.1.call-done, f32[3,256,256]{2,1,0:T(8,128)S(1)} %all_gather.10), kind=kOutput, calls=%fused_computation.7 | convolution fusion | flops 905969664 | bytes 3145728 | tf_op jit(solution)/shard_map/wpr,wrq->wpq/dot_general | solution.py:34
  90.5 0.0 all-gather.3.cloned.1.call-update
  90.5 0.0 copy-start.4
  90.5 0.0 all-reduce.3.cloned.1.call-start
  90.6 10.0 %all-gather.3.cloned.1.call-done = f32[3,256,768]{1,2,0:T(8,128)} async-done(((f32[3,256,384]{1,2,0:T(8,128)}), f32[3,256,768]{1,2,0:T(8,128)}) %all-gather.3.cloned.1.call-update) | async-done | bytes 2359312 | tf_op jit(solution)/shard_map/all_gather | solution.py:36
  100.6 25.5 %multiply_reduce_fusion = f32[3,2560]{1,0:T(4,128)S(1)} fusion(f32[3,256,768]{1,2,0:T(8,128)} %all-gather.3.cloned.1.call-done, f32[96,8,20,128]{3,2,1,0:T(8,128)} %bitcast.21, bf16[768,2560]{1,0:T(8,128)(2,1)} %param.7, f32[256,2560]{1,0:T(8,128)S(1)} %dynamic-slice_convert_fusion), kind=kOutput, calls=%fused_computation.2 | convolution fusion | flops 18127249408 | bytes 16807936 | tf_op jit(solution)/shard_map/tpq,qk->tpk/dot_general | solution.py:37
  126.1 0.0 copy-done
  126.1 1.0 fusion.7
  127.2 0.0 all-reduce.3.cloned.1.call-update
  127.2 0.0 copy-done.4
  127.2 0.6 dynamic-slice
  128.4 42.5 %all-reduce.3.cloned.1.call-done = f32[12,2560]{1,0:T(8,128)} async-done(((f32[12,2560]{1,0:T(8,128)}), f32[12,2560]{1,0:T(8,128)}) %all-reduce.3.cloned.1.call-update) | async-done | bytes 122896
  171.0 0.9 constant_dynamic-slice_fusion
  171.9 20.0 %psum.7 = f32[3,2560]{1,0:T(4,128)} all-reduce(f32[3,2560]{1,0:T(4,128)S(1)} %constant_dynamic-slice_fusion), channel_id=1, replica_groups=mesh['tm'=4,'aux'=4,'pair'=2] {'aux'}, use_global_device_ids=true, to_apply=%region_3.4 | all-reduce | flops 7680 | bytes 61440 | tf_op jit(solution)/shard_map/psum | solution.py:43
  (15 shorter events, 0.2 us)
Async XLA Ops:
  6.5 119.6 %copy-start = (f32[12,12]{1,0:T(8,128)S(1)}, f32[12,12]{1,0:T(8,128)}, u32[]{:S(2)}) copy-start(f32[12,12]{1,0:T(8,128)} %param.13) | copy-start | bytes 1732
  6.5 34.1 %copy-start.3 = (bf16[64,2560]{1,0:T(8,128)(2,1)S(1)}, bf16[64,2560]{1,0:T(8,128)(2,1)}, u32[]{:S(2)}) copy-start(bf16[64,2560]{1,0:T(8,128)(2,1)} %param.8) | copy-start | bytes 983044
  6.5 79.6 %reduce-scatter.2.cloned.1.call-start = ((), (), s32[]{:S(2)}) async-start(), calls=%async_computation.1 | async-start | bytes 3538944 | tf_op jit(solution)/shard_map/reduce_scatter | solution.py:32
  6.5 13.0 %collective-permute-start = (bf16[64,2560]{1,0:T(8,128)(2,1)}, bf16[64,2560]{1,0:T(8,128)(2,1)S(1)}, u32[]{:S(2)}, u32[]{:S(2)}) collective-permute-start(bf16[64,2560]{1,0:T(8,128)(2,1)} %param.8), channel_id=1, source_target_pairs={{0,2},{2,4},{4,6},{6,0},{1,3},{3,5},{5,7},{7,1},{8,10},{10,12},{12... | collective-permute-start | bytes 983048 | tf_op jit(solution)/shard_map/ppermute | solution.py:20
  19.6 10.7 %collective-permute-start.1 = (bf16[64,2560]{1,0:T(8,128)(2,1)S(1)}, bf16[64,2560]{1,0:T(8,128)(2,1)S(1)}, u32[]{:S(2)}, u32[]{:S(2)}) collective-permute-start(bf16[64,2560]{1,0:T(8,128)(2,1)S(1)} %collective-permute-done), channel_id=1, source_target_pairs={{0,2},{2,4},{4,6},{6,0},{1,3},{3,5},{5,7},{7,1},{8,10},{10,12},{12... | collective-permute-start | bytes 983048 | tf_op jit(solution)/shard_map/ppermute | solution.py:20
  30.2 10.3 %collective-permute-start.2 = (bf16[64,2560]{1,0:T(8,128)(2,1)S(1)}, bf16[64,2560]{1,0:T(8,128)(2,1)S(1)}, u32[]{:S(2)}, u32[]{:S(2)}) collective-permute-start(bf16[64,2560]{1,0:T(8,128)(2,1)S(1)} %collective-permute-done.1), channel_id=1, source_target_pairs={{0,2},{2,4},{4,6},{6,0},{1,3},{3,5},{5,7},{7,1},{8,10},{10,12},{12... | collective-permute-start | bytes 983048 | tf_op jit(solution)/shard_map/ppermute | solution.py:20
  41.1 4.4 %copy-start.2 = (bf16[768,2560]{1,0:T(8,128)(2,1)S(1)}, bf16[768,2560]{1,0:T(8,128)(2,1)}, u32[]{:S(2)}) copy-start(bf16[768,2560]{1,0:T(8,128)(2,1)} %param.7) | copy-start | bytes 11796484
  41.8 3.7 %copy-start.1 = (f32[6,128,20,128]{3,2,1,0:T(8,128)}, f32[6,128,20,128]{3,2,1,0:T(8,128)S(1)}, u32[]{:S(2)}) copy-start(f32[6,128,20,128]{3,2,1,0:T(8,128)S(1)} %broadcast_in_dim.2) | copy-start | bytes 23592964
  67.7 32.8 %all-gather.3.cloned.1.call-start = ((), (), s32[]{:S(2)}) async-start(), calls=%async_computation.2 | async-start | bytes 3538944 | tf_op jit(solution)/shard_map/all_gather | solution.py:36
  90.5 36.7 %copy-start.4 = (u32[32]{0:T(128)S(1)}, u32[32]{0:T(128)}, u32[]{:S(2)}) copy-start(u32[32]{0:T(128)} %constant.49) | copy-start | bytes 388
  90.5 80.4 %all-reduce.3.cloned.1.call-start = ((), (), s32[]{:S(2)}) async-start(), calls=%async_computation.3 | async-start | bytes 327680
Sparse Core Ops, SparseCore 0:
  67.9 10.4 reduce-scatter.1
  90.6 9.9 all-gather.2
  127.3 43.6 all-reduce.2
